TPU v7x, 512 devices: a whole 4x8x8 slice. The times are simulated.
512 devices in a mesh: section: 8 (over y), dp: 16 (over z, core), tensor: 4 (over x).
Axes of the slice: x: 4, y: 8, z: 8, core: 2. Of those that a mesh axis runs over, the one named last changes fastest.
Arguments:
- section_inputs: bfloat16 [8, 128, 2560], P('section', 'dp', 'tensor'), may hold values from -40 to 40
- entering: bfloat16 [1, 128, 2560], P(None, 'dp', 'tensor'), may hold values from -40 to 40
- grad_outputs: bfloat16 [8, 128, 2560], P('section', 'dp', 'tensor'), may hold values from -6 to 6
- arriving: bfloat16 [1, 128, 2560], P(None, 'dp', 'tensor'), may hold values from -6 to 6
- live_rows: int32 [1], replicated, may hold values from 64 to 128
- stashed_inputs: bfloat16 [8, 2, 128, 2560], P('section', None, 'dp', 'tensor'), may hold values from -40 to 40
- norm_gain: bfloat16 [8, 2560], P('section', 'tensor'), may hold values from 0.25 to 1.75
- up_weight: bfloat16 [8, 2560, 14336], P('section', 'tensor', 'dp'), may hold values from -0.125 to 0.125
- down_weight: bfloat16 [8, 14336, 2560], P('section', 'dp', 'tensor'), may hold values from -0.046875 to 0.046875
- held_blocks: int32 [8, 4, 16, 6], P('section', 'tensor'), may hold values from 0 to 69, as said below
- held_count: int32 [8, 4, 16], P('section', 'tensor'), may hold values from 1 to 6, as said below
- held_owner: int32 [8, 4, 16, 6], P('section', 'tensor'), may hold values from 0 to 15, as said below
- first_moment: float32 [8, 4, 16, 6, 128, 128], P('section', 'tensor', 'dp'), may hold values from -4 to 4
- second_moment: float32 [8, 4, 16, 6, 128, 128], P('section', 'tensor', 'dp'), may hold values from 0.01 to 1
Outputs:
- section_outputs: bfloat16 [8, 2, 128, 2560], P('section', None, 'dp', 'tensor')
- input_grads: bfloat16 [8, 2, 128, 2560], P('section', None, 'dp', 'tensor')
- first_next: float32 [8, 4, 16, 6, 128, 128], P('section', 'tensor', 'dp')
- second_next: float32 [8, 4, 16, 6, 128, 128], P('section', 'tensor', 'dp')
- update_direction: float32 [8, 4, 16, 6, 128, 128], P('section', 'tensor', 'dp')
Inputs may be any that keep to these rules, and one draw needn't show every extreme that they name: `held_blocks`: A number below 35 names a block of the device's up projection share, row-major over 5 x 7 blocks; the others, less 35, a block of its down projection share, row-major over 7 x 5 blocks. A device's first held_count entries are distinct; later entries are not used. `held_count`: some device of each section and tensor index lists 6 trainable blocks. `held_owner`: the owners of one device's trainable blocks are distinct and never the device itself. Each dp index owns at most 6 blocks of one section and tensor index, and some owns exactly 6.
All inputs are finite; a program needn't handle non-finite values.
Results may differ from a plain program's by a relative error of at most 0.015.
Values may be sent and summed in bfloat16 or wider, within the bound.
A program may use at most 64 MiB of HBM per device.

v0:
```python
import jax
import jax.numpy as jnp
from jax import lax
from jax.sharding import PartitionSpec as P

DW = 2560
BLK = 128
EPSILON = 1e-06


def from_behind(value, axis, steps):
    count = lax.axis_size(axis)
    leading, last = (max(0, -steps), min(count, count - steps))
    return lax.ppermute(value, axis, [(source, source + steps) for source in range(leading, last)])


def normed_product(rows_all, gain_row, up_matrix):
    widened = rows_all.astype(jnp.float32)
    squares = jnp.sum(widened * widened, axis=1)
    normed = (widened * gain_row.astype(jnp.float32)).astype(jnp.bfloat16)
    product = jnp.dot(normed, up_matrix, preferred_element_type=jnp.float32)
    return (normed, squares, product)


def scales_of(squares):
    return lax.rsqrt(squares / DW + EPSILON)


def activate(hidden):
    return (hidden * jax.nn.sigmoid(hidden)).astype(jnp.bfloat16)


def hidden_backward(hidden, act_grad, row_scales, product):
    sigmoid_part = jax.nn.sigmoid(hidden)
    hidden_grad = act_grad * sigmoid_part * (1.0 + hidden * (1.0 - sigmoid_part))
    scaled_grad = (hidden_grad * row_scales[:, None]).astype(jnp.bfloat16)
    scale_grad = jnp.sum(hidden_grad * product, axis=1)
    return (scaled_grad, scale_grad)


def times_transposed(left, right):
    return lax.dot_general(
        left, right, (((1,), (1,)), ((), ())), preferred_element_type=jnp.float32
    )


def body(
    section_inputs,
    entering,
    grad_outputs,
    arriving,
    live_rows,
    stashed_inputs,
    norm_gain,
    up_weight,
    down_weight,
    held_blocks,
    held_count,
    held_owner,
    first_moment,
    second_moment,
):
    section_count = lax.axis_size("section")
    section_index = lax.axis_index("section")
    dp_index = lax.axis_index("dp")
    dp_count = lax.axis_size("dp")
    turn_count = stashed_inputs.shape[1]
    local_rows = section_inputs.shape[1]
    row_total = local_rows * dp_count
    gain_row = norm_gain[0]
    up_matrix = up_weight[0]
    down_matrix = down_weight[0]
    channel_blocks = up_matrix.shape[0] // BLK
    hidden_blocks = up_matrix.shape[1] // BLK
    up_count = channel_blocks * hidden_blocks
    capacity = held_owner.shape[3]
    row_start = dp_index * local_rows
    held_list = lax.dynamic_index_in_dim(held_blocks[0, 0], dp_index, 0, keepdims=False)
    down_number = held_list - up_count
    is_up = held_list < up_count
    left_index = jnp.where(
        is_up, held_list // hidden_blocks, channel_blocks + down_number // channel_blocks
    )
    right_index = jnp.where(
        is_up, held_list % hidden_blocks, hidden_blocks + down_number % channel_blocks
    )
    forward_results = []
    rows_in = section_inputs[0]
    for turn in range(turn_count):
        if turn > 0:
            passed_rows = from_behind(forward_results[-1], "section", 1)
            rows_in = jnp.where(section_index == 0, entering[turn - 1], passed_rows)
        forward_rows_all = lax.all_gather(rows_in, "dp", axis=0, tiled=True)
        forward_normed, forward_squares, forward_product = normed_product(
            forward_rows_all, gain_row, up_matrix
        )
        forward_product, forward_squares = (
            lax.psum(forward_product.astype(jnp.bfloat16), "tensor").astype(jnp.float32),
            lax.psum(forward_squares.astype(jnp.bfloat16), "tensor").astype(jnp.float32),
        )
        forward_activated = activate(forward_product * scales_of(forward_squares)[:, None])
        mixed_rows = lax.psum_scatter(
            jnp.dot(forward_activated, down_matrix, preferred_element_type=jnp.float32).astype(
                jnp.bfloat16
            ),
            "dp",
            scatter_dimension=0,
            tiled=True,
        ).astype(jnp.float32)
        forward_results.append((rows_in.astype(jnp.float32) + mixed_rows).astype(jnp.bfloat16))
    row_ids = row_start + lax.iota(jnp.int32, local_rows)
    backward_results = []
    kept_grads = jnp.zeros((capacity, BLK, BLK), jnp.float32)
    grads_in = grad_outputs[0]
    for turn in range(turn_count):
        if turn > 0:
            passed_grads = from_behind(backward_results[-1], "section", -1)
            masked = jnp.where(
                (row_ids < live_rows[turn - 1])[:, None],
                arriving[turn - 1],
                jnp.zeros_like(arriving[turn - 1]),
            )
            grads_in = jnp.where(section_index == section_count - 1, masked, passed_grads)
        rows_local = stashed_inputs[0, turn]
        rows_all = lax.all_gather(rows_local, "dp", axis=0, tiled=True)
        grads_all = lax.all_gather(grads_in, "dp", axis=0, tiled=True)
        normed, squares, product = normed_product(rows_all, gain_row, up_matrix)
        act_grad = times_transposed(grads_all, down_matrix)
        product, squares, act_grad = lax.psum((product, squares, act_grad), "tensor")
        row_scales = scales_of(squares)
        hidden = product * row_scales[:, None]
        activated = activate(hidden)
        scaled_grad, scale_grad = hidden_backward(hidden, act_grad, row_scales, product)
        normed_part = times_transposed(scaled_grad, up_matrix)
        normed_grad = lax.psum_scatter(normed_part, "dp", scatter_dimension=0, tiled=True)
        scale_grad_rows = lax.psum_scatter(scale_grad, "dp", scatter_dimension=0, tiled=True)
        scale_rows = lax.dynamic_slice_in_dim(row_scales, row_start, local_rows, 0)
        widened = rows_local.astype(jnp.float32)
        input_grad = (
            grads_in.astype(jnp.float32)
            + normed_grad * gain_row.astype(jnp.float32)
            - (scale_grad_rows * scale_rows**3)[:, None] * widened / DW
        )
        left_table = jnp.concatenate(
            [
                normed.reshape(row_total, channel_blocks, BLK),
                activated.reshape(row_total, hidden_blocks, BLK),
            ],
            axis=1,
        )
        right_table = jnp.concatenate(
            [
                scaled_grad.reshape(row_total, hidden_blocks, BLK),
                grads_all.reshape(row_total, channel_blocks, BLK),
            ],
            axis=1,
        )
        left_pick = jnp.take(left_table, left_index, axis=1)
        right_pick = jnp.take(right_table, right_index, axis=1)
        block_grads = jnp.einsum(
            "rkb,rkc->kbc", left_pick, right_pick, preferred_element_type=jnp.float32
        )
        result, block_grads = (input_grad.astype(jnp.bfloat16), block_grads)
        backward_results.append(result)
        kept_grads = kept_grads + block_grads
    counts = held_count[0, 0]
    owners = held_owner[0, 0]
    slot_ids = lax.iota(jnp.int32, capacity)
    dp_ids = lax.iota(jnp.int32, dp_count)
    live_slots = slot_ids[None, :] < counts[:, None]
    chosen = (owners[:, None, :] == dp_ids[None, :, None]) & live_slots[:, None, :]
    is_sent = jnp.any(chosen, axis=2)
    slot_pick = jnp.sum(jnp.where(chosen, slot_ids[None, None, :], 0), axis=2)
    mine_sent = lax.dynamic_index_in_dim(is_sent, dp_index, 0, keepdims=False)
    mine_pick = lax.dynamic_index_in_dim(slot_pick, dp_index, 0, keepdims=False)
    outgoing = jnp.where(mine_sent[:, None, None], jnp.take(kept_grads, mine_pick, axis=0), 0.0)
    arrived = lax.all_to_all(outgoing, "dp", split_axis=0, concat_axis=0, tiled=True)
    from_source = lax.dynamic_index_in_dim(is_sent, dp_index, 1, keepdims=False)
    source_count = from_source.astype(jnp.int32)
    ranks = jnp.cumsum(source_count) - source_count
    matches = from_source[None, :] & (ranks[None, :] == slot_ids[:, None])
    is_filled = jnp.any(matches, axis=1)
    source_ids = jnp.sum(jnp.where(matches, dp_ids[None, :], 0), axis=1)
    owned_grads = jnp.where(is_filled[:, None, None], jnp.take(arrived, source_ids, axis=0), 0.0)
    filled = is_filled[:, None, None]
    first_new = 0.9 * first_moment[0, 0, 0] + 0.1 * owned_grads
    second_new = 0.999 * second_moment[0, 0, 0] + 0.001 * owned_grads * owned_grads
    direction = first_new / (jnp.sqrt(second_new) + 1e-08)
    first_out = jnp.where(filled, first_new, 0.0)
    second_out = jnp.where(filled, second_new, 0.0)
    direction_out = jnp.where(filled, direction, 0.0)
    section_rows = jnp.stack(forward_results)
    grad_rows = jnp.stack(backward_results)
    return (
        section_rows[None],
        grad_rows[None],
        first_out[None, None, None],
        second_out[None, None, None],
        direction_out[None, None, None],
    )


def solution(mesh):
    return jax.shard_map(
        body,
        mesh=mesh,
        in_specs=(
            P("section", "dp", "tensor"),
            P(None, "dp", "tensor"),
            P("section", "dp", "tensor"),
            P(None, "dp", "tensor"),
            P(),
            P("section", None, "dp", "tensor"),
            P("section", "tensor"),
            P("section", "tensor", "dp"),
            P("section", "dp", "tensor"),
            P("section", "tensor", None, None),
            P("section", "tensor", None),
            P("section", "tensor", None, None),
            P("section", "tensor", "dp", None, None, None),
            P("section", "tensor", "dp", None, None, None),
        ),
        out_specs=(
            P("section", None, "dp", "tensor"),
            P("section", None, "dp", "tensor"),
            P("section", "tensor", "dp", None, None, None),
            P("section", "tensor", "dp", None, None, None),
            P("section", "tensor", "dp", None, None, None),
        ),
        check_vma=False,
    )
```

profile of v0, /device:TPU:1, one launch (start us, length us, event | category | flops | bytes accessed | tf_op | source)
XLA Modules:
  0.0 778.5 jit_solution(2961250332882547614)
XLA Ops:
  7.2 0.8 convert_reduce_fusion
  8.8 24.9 %all-gather.2 = bf16[1,1,128,640]{3,2,1,0:T(8,128)(2,1)S(1)} all-gather(bf16[1,1,8,640]{3,2,1,0:T(8,128)(2,1)S(1)} %get-tuple-element.41), channel_id=4, replica_groups=mesh['section'=8,'dp'=16,'tensor'=4] {'dp'}, dimensions={2}, use_global_device_ids=true | all-gather | bytes 174080 | tf_op jit(solution)/shard_map/all_gather | solution.py:125
  33.9 15.2 %all-gather.1 = bf16[1,128,640]{2,1,0:T(8,128)(2,1)S(1)} all-gather(bf16[1,8,640]{2,1,0:T(8,128)(2,1)} %param.18), channel_id=3, replica_groups=mesh['section'=8,'dp'=16,'tensor'=4] {'dp'}, dimensions={1}, use_global_device_ids=true | all-gather | bytes 174080 | tf_op jit(solution)/shard_map/all_gather | solution.py:126
  49.0 16.2 %all-gather.3 = bf16[1,1,128,640]{3,2,1,0:T(8,128)(2,1)S(1)} all-gather(bf16[1,1,8,640]{3,2,1,0:T(8,128)(2,1)S(1)} %get-tuple-element.42), channel_id=5, replica_groups=mesh['section'=8,'dp'=16,'tensor'=4] {'dp'}, dimensions={2}, use_global_device_ids=true | all-gather | bytes 174080 | tf_op jit(solution)/shard_map/all_gather | solution.py:125
  65.4 1.2 fusion.2
  66.8 1.2 fusion.12
  68.1 14.9 %all-gather = bf16[1,128,640]{2,1,0:T(8,128)(2,1)S(1)} all-gather(bf16[1,8,640]{2,1,0:T(8,128)(2,1)S(1)} %copy-done.15), channel_id=2, replica_groups=mesh['section'=8,'dp'=16,'tensor'=4] {'dp'}, dimensions={1}, use_global_device_ids=true | all-gather | bytes 174080 | tf_op jit(solution)/shard_map/all_gather | solution.py:93
  83.2 8.9 %all-reduce.6 = (f32[128]{0:T(128)S(1)}, f32[128]{0:T(128)S(1)}) all-reduce(f32[128]{0:T(128)S(1)} %get-tuple-element.38, f32[128]{0:T(128)S(1)} %get-tuple-element.43), channel_id=1, replica_groups=mesh['section'=8,'dp'=16,'tensor'=4] {'tensor'}, use_global_device_ids=true, to_apply=%region_18.19 | all-reduce | flops 256 | bytes 2048 | tf_op jit(solution)/shard_map/psum | solution.py:129
  92.1 27.8 %all-reduce.32.cloned.1.call-done = (f32[128,896]{1,0:T(8,128)}, f32[128,896]{1,0:T(8,128)}) async-done(((f32[128,896]{1,0:T(8,128)}, f32[128,896]{1,0:T(8,128)}), (f32[128,896]{1,0:T(8,128)}, f32[128,896]{1,0:T(8,128)})) %all-reduce.32.cloned.1.call-update) | async-done | bytes 917520 | tf_op jit(solution)/shard_map/psum | solution.py:129
  119.9 1.6 multiply_reduce_fusion.1
  121.4 1.2 fusion.10
  122.7 1.3 convolution_convert_fusion.1
  129.6 8.1 %psum.71 = bf16[128]{0:T(256)(128)(2,1)S(1)} all-reduce(bf16[128]{0:T(256)(128)(2,1)S(1)} %fusion.21), channel_id=1, replica_groups=mesh['section'=8,'dp'=16,'tensor'=4] {'tensor'}, use_global_device_ids=true, to_apply=%region_2.3 | all-reduce | flops 128 | bytes 512 | tf_op jit(solution)/shard_map/psum | solution.py:99
  137.6 1.2 fusion.8
  138.8 1.3 dynamic-slice.1
  140.8 28.0 %all-reduce.3 = f32[128]{0:T(128)S(1)} all-reduce(f32[128]{0:T(128)S(1)} %get-tuple-element.30), channel_id=9, replica_groups=mesh['section'=8,'dp'=16,'tensor'=4] {'dp'}, use_global_device_ids=true, to_apply=%region_14.15.clone | all-reduce | flops 128 | bytes 1024
  168.9 69.6 %all-reduce.26.cloned.1.call-done = f32[128,640]{1,0:T(8,128)} async-done(((f32[128,640]{1,0:T(8,128)}), f32[128,640]{1,0:T(8,128)}) %all-reduce.26.cloned.1.call-update) | async-done | bytes 327696
  239.4 1.4 collective-permute-start.1
  240.8 50.0 %all-reduce.18.cloned.1.call-done = bf16[128,896]{1,0:T(8,128)(2,1)} async-done(((bf16[128,896]{1,0:T(8,128)(2,1)}), bf16[128,896]{1,0:T(8,128)(2,1)}) %all-reduce.18.cloned.1.call-update) | async-done | bytes 229392 | tf_op jit(solution)/shard_map/psum | solution.py:98
  290.8 2.0 convolution_convert_fusion.3
  293.0 21.1 %all_gather.22 = bf16[128,640]{1,0:T(8,128)(2,1)S(1)} all-gather(bf16[8,640]{1,0:T(8,128)(2,1)S(1)} %fusion.63), channel_id=1, replica_groups=mesh['section'=8,'dp'=16,'tensor'=4] {'dp'}, dimensions={0}, use_global_device_ids=true | all-gather | bytes 174080 | tf_op jit(solution)/shard_map/all_gather | solution.py:126
  314.8 1.3 fusion
  316.0 88.5 %all-reduce.22.cloned.1.call-done = bf16[128,640]{1,0:T(8,128)(2,1)} async-done(((bf16[128,640]{1,0:T(8,128)(2,1)}), bf16[128,640]{1,0:T(8,128)(2,1)}) %all-reduce.22.cloned.1.call-update) | async-done | bytes 163856
  405.3 3.1 collective-permute-start
  411.6 16.2 %all_gather.19 = bf16[128,640]{1,0:T(8,128)(2,1)S(1)} all-gather(bf16[8,640]{1,0:T(8,128)(2,1)S(1)} %bitcast_select_fusion.2), channel_id=1, replica_groups=mesh['section'=8,'dp'=16,'tensor'=4] {'dp'}, dimensions={0}, use_global_device_ids=true | all-gather | bytes 174080 | tf_op jit(solution)/shard_map/all_gather | solution.py:93
  428.4 0.8 copy.100
  429.4 1.1 pad_maximum_fusion
  431.1 1.0 pad_maximum_fusion.1
  434.0 26.0 %all-reduce.30.cloned.1.call-done = (f32[128,896]{1,0:T(8,128)}, f32[128,896]{1,0:T(8,128)}) async-done(((f32[128,896]{1,0:T(8,128)}, f32[128,896]{1,0:T(8,128)}), (f32[128,896]{1,0:T(8,128)}, f32[128,896]{1,0:T(8,128)})) %all-reduce.30.cloned.1.call-update) | async-done | bytes 917520 | tf_op jit(solution)/shard_map/psum | solution.py:129
  460.1 2.1 multiply_reduce_fusion
  463.2 1.1 pad_maximum_fusion.2
  464.3 1.4 gather_fusion.4
  466.7 1.1 pad_maximum_fusion.3
  467.7 1.4 gather_fusion.5
  469.1 1.4 convolution_add_fusion
  470.5 1.8 gather_fusion
  472.3 2.5 select_select_fusion
  474.7 9.7 %all-to-all-start = ((f32[16,128,128]{2,1,0:T(8,128)}), f32[16,128,128]{2,1,0:T(8,128)}, u32[]{:S(2)}, u32[]{:S(2)}) async-start(f32[16,128,128]{2,1,0:T(8,128)} %select_select_fusion), calls=%async_computation | async-start | bytes 2097152 | tf_op jit(solution)/shard_map/all_to_all | solution.py:177
  484.5 1.3 convolution_convert_fusion
  485.9 8.5 %psum.73 = bf16[128]{0:T(256)(128)(2,1)S(1)} all-reduce(bf16[128]{0:T(256)(128)(2,1)S(1)} %fusion.19), channel_id=1, replica_groups=mesh['section'=8,'dp'=16,'tensor'=4] {'tensor'}, use_global_device_ids=true, to_apply=%region_6.7 | all-reduce | flops 128 | bytes 512 | tf_op jit(solution)/shard_map/psum | solution.py:99
  494.4 43.6 %all-reduce.20.cloned.1.call-done = bf16[128,896]{1,0:T(8,128)(2,1)} async-done(((bf16[128,896]{1,0:T(8,128)(2,1)}), bf16[128,896]{1,0:T(8,128)(2,1)}) %all-reduce.20.cloned.1.call-update) | async-done | bytes 229392 | tf_op jit(solution)/shard_map/psum | solution.py:98
  538.1 2.0 convolution_convert_fusion.2
  540.2 111.8 %all-reduce.24.cloned.1.call-done = bf16[128,640]{1,0:T(8,128)(2,1)} async-done(((bf16[128,640]{1,0:T(8,128)(2,1)}), bf16[128,640]{1,0:T(8,128)(2,1)}) %all-reduce.24.cloned.1.call-update) | async-done | bytes 163856
  652.7 1.2 fusion.6
  654.6 23.2 %all-reduce.5 = f32[128]{0:T(128)S(1)} all-reduce(f32[128]{0:T(128)S(1)} %copy-done.28), channel_id=11, replica_groups=mesh['section'=8,'dp'=16,'tensor'=4] {'dp'}, use_global_device_ids=true, to_apply=%region_21.22.clone | all-reduce | flops 128 | bytes 1024
  677.8 89.3 %all-reduce.28.cloned.1.call-done = f32[128,640]{1,0:T(8,128)} async-done(((f32[128,640]{1,0:T(8,128)}), f32[128,640]{1,0:T(8,128)}) %all-reduce.28.cloned.1.call-update) | async-done | bytes 327696
  768.5 1.8 gather_fusion.1
  770.4 1.3 divide_select_fusion
  (149 shorter events, 20.4 us)
Async XLA Ops:
  7.2 59.6 %copy-start = (bf16[1,640,896]{2,1,0:T(8,128)(2,1)S(1)}, bf16[1,640,896]{2,1,0:T(8,128)(2,1)}, u32[]{:S(2)}) copy-start(bf16[1,640,896]{2,1,0:T(8,128)(2,1)} %param.23) | copy-start | bytes 3440644
  7.2 58.2 %copy-start.1 = (bf16[1,896,640]{2,1,0:T(8,128)(2,1)S(1)}, bf16[1,896,640]{2,1,0:T(8,128)(2,1)}, u32[]{:S(2)}) copy-start(bf16[1,896,640]{2,1,0:T(8,128)(2,1)} %param.24) | copy-start | bytes 3440644
  7.2 112.7 %all-reduce.32.cloned.1.call-start = ((), (), s32[]{:S(2)}) async-start(), calls=%async_computation.8 | async-start | bytes 1835008 | tf_op jit(solution)/shard_map/psum | solution.py:129
  66.8 1.3 copy-start.15
  68.0 170.5 %all-reduce.26.cloned.1.call-start = ((), (), s32[]{:S(2)}) async-start(), calls=%async_computation.5 | async-start | bytes 655360
  122.6 1.4 copy-start.16
  122.6 2.5 copy-start.34
  122.6 2.6 copy-start.25
  122.7 168.1 %all-reduce.18.cloned.1.call-start = ((), (), s32[]{:S(2)}) async-start(), calls=%async_computation.1 | async-start | bytes 458752 | tf_op jit(solution)/shard_map/psum | solution.py:98
  124.0 114.6 %copy-start.8 = (bf16[1,2,8,640]{3,2,1,0:T(8,128)(2,1)S(1)}, bf16[1,2,8,640]{3,2,1,0:T(8,128)(2,1)}, u32[]{:S(2)}) copy-start(bf16[1,2,8,640]{3,2,1,0:T(8,128)(2,1)} %param.21) | copy-start | bytes 61444
  124.0 114.6 %copy-start.14 = (bf16[1,8,640]{2,1,0:T(8,128)(2,1)S(1)}, bf16[1,8,640]{2,1,0:T(8,128)(2,1)}, u32[]{:S(2)}) copy-start(bf16[1,8,640]{2,1,0:T(8,128)(2,1)} %param.18) | copy-start | bytes 30724
  124.0 280.6 %all-reduce.22.cloned.1.call-start = ((), (), s32[]{:S(2)}) async-start(), calls=%async_computation.3 | async-start | bytes 327680
  129.6 330.5 %copy-start.26 = (f32[128]{0:T(128)}, f32[128]{0:T(128)S(1)}, u32[]{:S(2)}) copy-start(f32[128]{0:T(128)S(1)} %add_rsqrt_fusion) | copy-start | bytes 1540
  140.8 291.9 %copy-start.21 = (pred[6]{0:T(512)(128)(4,1)}, pred[6]{0:T(512)(128)(4,1)S(1)}, u32[]{:S(2)}) copy-start(pred[6]{0:T(512)(128)(4,1)S(1)} %get-tuple-element.24) | copy-start | bytes 22
  140.8 291.9 %copy-start.23 = (pred[6]{0:T(512)(128)(4,1)}, pred[6]{0:T(512)(128)(4,1)S(1)}, u32[]{:S(2)}) copy-start(pred[6]{0:T(512)(128)(4,1)S(1)} %get-tuple-element.47) | copy-start | bytes 22
  140.8 289.7 %copy-start.20 = (s32[1024]{0:T(1024)}, s32[1024]{0:T(1024)S(1)}, u32[]{:S(2)}) copy-start(s32[1024]{0:T(1024)S(1)} %get-tuple-element.50) | copy-start | bytes 12292
  140.8 291.3 %copy-start.19 = (s32[1024]{0:T(1024)}, s32[1024]{0:T(1024)S(1)}, u32[]{:S(2)}) copy-start(s32[1024]{0:T(1024)S(1)} %get-tuple-element.49) | copy-start | bytes 12292
  239.4 53.5 %copy-start.10 = (bf16[8,640]{1,0:T(8,128)(2,1)}, bf16[8,640]{1,0:T(8,128)(2,1)S(1)}, u32[]{:S(2)}) copy-start(bf16[8,640]{1,0:T(8,128)(2,1)S(1)} %fusion.58) | copy-start | bytes 30724
  239.4 53.5 %copy-start.17 = (bf16[1,8,640]{2,1,0:T(8,128)(2,1)S(1)}, bf16[1,8,640]{2,1,0:T(8,128)(2,1)}, u32[]{:S(2)}) copy-start(bf16[1,8,640]{2,1,0:T(8,128)(2,1)} %param.19) | copy-start | bytes 30724
  239.4 53.5 %collective-permute-start.1 = (bf16[8,640]{1,0:T(8,128)(2,1)S(1)}, bf16[8,640]{1,0:T(8,128)(2,1)S(1)}, u32[]{:S(2)}, u32[]{:S(2)}) collective-permute-start(bf16[8,640]{1,0:T(8,128)(2,1)S(1)} %fusion.58), channel_id=1, source_target_pairs={{64,0},{128,64},{192,128},{256,192},{320,256},{384,320},{448,384},... | collective-permute-start | bytes 30728 | tf_op jit(solution)/shard_map/ppermute | solution.py:14
  292.8 167.2 %all-reduce.30.cloned.1.call-start = ((), (), s32[]{:S(2)}) async-start(), calls=%async_computation.7 | async-start | bytes 1835008 | tf_op jit(solution)/shard_map/psum | solution.py:129
  314.1 0.7 copy-start.2
  316.0 95.6 %copy-start.18 = (bf16[1,8,640]{2,1,0:T(8,128)(2,1)S(1)}, bf16[1,8,640]{2,1,0:T(8,128)(2,1)}, u32[]{:S(2)}) copy-start(bf16[1,8,640]{2,1,0:T(8,128)(2,1)} %param.17) | copy-start | bytes 30724
  405.3 6.3 copy-start.12
  405.3 6.3 collective-permute-start
  411.6 17.6 %copy-start.6 = (bf16[8,640]{1,0:T(8,128)(2,1)}, bf16[8,640]{1,0:T(8,128)(2,1)S(1)}, u32[]{:S(2)}) copy-start(bf16[8,640]{1,0:T(8,128)(2,1)S(1)} %bitcast_select_fusion.2) | copy-start | bytes 30724
  431.1 2.0 copy-start.3
  465.6 3.5 copy-start.22
  465.6 3.5 copy-start.24
  470.5 1.8 copy-start.32
  470.5 1.8 copy-start.33
  474.7 293.8 %all-to-all-start = ((f32[16,128,128]{2,1,0:T(8,128)}), f32[16,128,128]{2,1,0:T(8,128)}, u32[]{:S(2)}, u32[]{:S(2)}) async-start(f32[16,128,128]{2,1,0:T(8,128)} %select_select_fusion), calls=%async_computation | async-start | bytes 2097152 | tf_op jit(solution)/shard_map/all_to_all | solution.py:177
  484.4 53.7 %all-reduce.20.cloned.1.call-start = ((), (), s32[]{:S(2)}) async-start(), calls=%async_computation.2 | async-start | bytes 458752 | tf_op jit(solution)/shard_map/psum | solution.py:98
  485.7 166.3 %all-reduce.24.cloned.1.call-start = ((), (), s32[]{:S(2)}) async-start(), calls=%async_computation.4 | async-start | bytes 327680
  494.4 45.8 %copy-start.29 = (s32[6]{0:T(128)S(1)}, s32[6]{0:T(128)}, u32[]{:S(2)}) copy-start(s32[6]{0:T(128)} %fusion.72) | copy-start | bytes 76
  494.4 157.6 %copy-start.7 = (bf16[8,640]{1,0:T(8,128)(2,1)S(1)}, bf16[8,640]{1,0:T(8,128)(2,1)}, u32[]{:S(2)}) copy-start(bf16[8,640]{1,0:T(8,128)(2,1)} %copy-done.6) | copy-start | bytes 30724
  540.1 113.8 %copy-start.13 = (bf16[8,640]{1,0:T(8,128)(2,1)S(1)}, bf16[8,640]{1,0:T(8,128)(2,1)}, u32[]{:S(2)}) copy-start(bf16[8,640]{1,0:T(8,128)(2,1)} %copy-done.12) | copy-start | bytes 30724
  540.1 114.5 %copy-start.28 = (f32[128]{0:T(128)S(1)}, f32[128]{0:T(128)}, u32[]{:S(2)}) copy-start(f32[128]{0:T(128)} %get-tuple-element.28) | copy-start | bytes 1540
  540.1 137.6 %copy-start.27 = (f32[128]{0:T(128)S(1)}, f32[128]{0:T(128)}, u32[]{:S(2)}) copy-start(f32[128]{0:T(128)} %copy-done.26) | copy-start | bytes 1540
  540.1 227.0 %copy-start.9 = (bf16[1,2,8,640]{3,2,1,0:T(8,128)(2,1)S(1)}, bf16[1,2,8,640]{3,2,1,0:T(8,128)(2,1)}, u32[]{:S(2)}) copy-start(bf16[1,2,8,640]{3,2,1,0:T(8,128)(2,1)} %param.21) | copy-start | bytes 61444
  540.1 227.8 %copy-start.11 = (bf16[8,640]{1,0:T(8,128)(2,1)S(1)}, bf16[8,640]{1,0:T(8,128)(2,1)}, u32[]{:S(2)}) copy-start(bf16[8,640]{1,0:T(8,128)(2,1)} %copy-done.10) | copy-start | bytes 30724
  540.2 226.9 %all-reduce.28.cloned.1.call-start = ((), (), s32[]{:S(2)}) async-start(), calls=%async_computation.6 | async-start | bytes 655360
  652.7 117.6 %copy-start.4 = (f32[1,1,1,6,128,128]{5,4,3,2,1,0:T(8,128)S(1)}, f32[1,1,1,6,128,128]{5,4,3,2,1,0:T(8,128)}, u32[]{:S(2)}) copy-start(f32[1,1,1,6,128,128]{5,4,3,2,1,0:T(8,128)} %param.28) | copy-start | bytes 1179652
  652.7 117.6 %copy-start.5 = (f32[1,1,1,6,128,128]{5,4,3,2,1,0:T(8,128)S(1)}, f32[1,1,1,6,128,128]{5,4,3,2,1,0:T(8,128)}, u32[]{:S(2)}) copy-start(f32[1,1,1,6,128,128]{5,4,3,2,1,0:T(8,128)} %param.29) | copy-start | bytes 1179652
  652.7 117.6 %copy-start.30 = (pred[6]{0:T(512)(128)(4,1)S(1)}, pred[6]{0:T(512)(128)(4,1)}, u32[]{:S(2)}) copy-start(pred[6]{0:T(512)(128)(4,1)} %fusion.65) | copy-start | bytes 22
  652.7 117.6 %copy-start.31 = (pred[6]{0:T(512)(128)(4,1)S(1)}, pred[6]{0:T(512)(128)(4,1)}, u32[]{:S(2)}) copy-start(pred[6]{0:T(512)(128)(4,1)} %compare_and_fusion.3) | copy-start | bytes 22
Sparse Core Ops, SparseCore 0:
  68.2 51.6 all-reduce.31
  122.8 115.7 all-reduce.25
  241.6 49.1 all-reduce.17
  293.5 110.9 all-reduce.21
  406.9 53.0 all-reduce.29
  487.9 50.0 all-reduce.19
  541.0 110.9 all-reduce.23
  655.0 112.0 all-reduce.27
where the time goes:
time: 779 us; the launch traced here: 778 us
  waiting for transfers between devices  507 us (65%)
  blocking collectives  185 us (24%)
  other arithmetic  22 us (3%)
  local copies, waits for them, and re-layouts  18.4 us (2%)
  between operations  16 us (2%)
  matrix products  15.5 us (2%)
  starting transfers between devices  14.6 us (2%)
    unnamed x12, waiting for transfers between devices  359 us
    psum x2, waiting for transfers between devices, body(): lax.psum(forward_product.astype(jnp.bfloat16), 'tensor').astype(jnp.float32)  93.6 us
    psum x2, waiting for transfers between devices, body(): lax.psum((product, squares, act_grad), 'tensor')  53.8 us
    unnamed x2, blocking collectives  51.2 us
    all_gather x2, blocking collectives, body(): rows_all = lax.all_gather(rows_local, 'dp', axis=0, tiled=True)  41.1 us
    all_gather x2, blocking collectives, body(): grads_all = lax.all_gather(grads_in, 'dp', axis=0, tiled=True)  36.3 us
    all_gather x2, blocking collectives, body(): forward_rows_all = lax.all_gather(rows_in, 'dp', axis=0, tiled=True)  31.2 us
    psum x2, blocking collectives, body(): lax.psum(forward_squares.astype(jnp.bfloat16), 'tensor').astype(jnp.float32)  16.6 us
  transfers between devices with their start and end apart: 11, of which 8 were waited for; matrix products, arithmetic and copies ran while one was open for 4% of the time, Pallas kernels for 0%

commit v1 on v0

--- a/solution.py
+++ b/solution.py
@@ -123,7 +123,14 @@
             grads_in = jnp.where(section_index == section_count - 1, masked, passed_grads)
         rows_local = stashed_inputs[0, turn]
         rows_all = lax.all_gather(rows_local, "dp", axis=0, tiled=True)
-        grads_all = lax.all_gather(grads_in, "dp", axis=0, tiled=True)
+        ring = [grads_in]
+        for hop in range(15):
+            ring.append(lax.ppermute(ring[-1], "dp", [(dev, (dev + 1) % 16) for dev in range(16)]))
+        grads_all = jnp.roll(
+            jnp.concatenate(ring[::-1], axis=0),
+            (lax.axis_index("dp") + 1) * ring[0].shape[0],
+            axis=0,
+        )
         normed, squares, product = normed_product(rows_all, gain_row, up_matrix)
         act_grad = times_transposed(grads_all, down_matrix)
         product, squares, act_grad = lax.psum((product, squares, act_grad), "tensor")

time: 779 us -> 833 us (1.069)
  waiting for transfers between devices: 507 us -> 585 us
  blocking collectives: 185 us -> 143 us
  starting transfers between devices: 14.6 us -> 26.9 us
    ppermute x0 -> x30, waiting for transfers between devices: none -> 96.9 us  [body(): lax.ppermute(ring[-1], 'dp', [(dev, (dev + 1) % 16) for dev in range(16)])]
    psum x2, waiting for transfers between devices: 93.6 us -> 43.6 us  [body(): lax.psum(forward_product.astype(jnp.bfloat16), 'tensor').astype(jnp.float32)]
    all_gather x2 -> x0, blocking collectives: 36.3 us -> none  [body(): grads_all = lax.all_gather(grads_in, 'dp', axis=0, tiled=True)]
    unnamed x12, waiting for transfers between devices: 359 us -> 388 us
    ppermute x0 -> x30, starting transfers between devices: none -> 12.5 us  [body(): lax.ppermute(ring[-1], 'dp', [(dev, (dev + 1) % 16) for dev in range(16)])]
  transfers between devices with their start and end apart: 11 -> 41, of which waited for: 8 -> 35; matrix products, arithmetic and copies ran while one was open for 4% -> 4% of each run, Pallas kernels for 0% -> 0%
where the time goes in v1:
time: 833 us; the launch traced here: 832 us
  waiting for transfers between devices  585 us (70%)
  blocking collectives  143 us (17%)
  starting transfers between devices  26.9 us (3%)
  other arithmetic  23.6 us (3%)
  local copies, waits for them, and re-layouts  20.8 us (2%)
  matrix products  16.5 us (2%)
  between operations  16 us (2%)
    unnamed x12, waiting for transfers between devices  388 us
    ppermute x30, waiting for transfers between devices, body(): lax.ppermute(ring[-1], 'dp', [(dev, (dev + 1) % 16) for dev in range(16)])  96.9 us
    psum x2, waiting for transfers between devices, body(): lax.psum((product, squares, act_grad), 'tensor')  53.5 us
    unnamed x2, blocking collectives  49.5 us
    psum x2, waiting for transfers between devices, body(): lax.psum(forward_product.astype(jnp.bfloat16), 'tensor').astype(jnp.float32)  43.6 us
    all_gather x2, blocking collectives, body(): forward_rows_all = lax.all_gather(rows_in, 'dp', axis=0, tiled=True)  34.3 us
    all_gather x2, blocking collectives, body(): rows_all = lax.all_gather(rows_local, 'dp', axis=0, tiled=True)  33.2 us
    psum x2, blocking collectives, body(): lax.psum(forward_squares.astype(jnp.bfloat16), 'tensor').astype(jnp.float32)  16.9 us
  transfers between devices with their start and end apart: 41, of which 35 were waited for; matrix products, arithmetic and copies ran while one was open for 4% of the time, Pallas kernels for 0%

profile of v1, /device:TPU:1, one launch (start us, length us, event | category | flops | bytes accessed | tf_op | source)
XLA Modules:
  0.0 832.3 jit_solution(2538199378248659921)
XLA Ops:
  7.2 3.5 collective-permute-start.1
  10.7 4.3 collective-permute-done.1
  15.0 4.5 collective-permute-done.2
  19.5 4.3 collective-permute-done.3
  23.8 4.3 collective-permute-done.4
  28.1 4.3 collective-permute-done.5
  32.4 4.3 collective-permute-done.6
  36.7 4.3 collective-permute-done.7
  41.0 4.3 collective-permute-done.8
  45.3 4.3 collective-permute-done.9
  50.4 3.6 collective-permute-done.10
  54.6 3.6 collective-permute-done.11
  58.3 18.1 %all-gather.1 = bf16[1,1,128,640]{3,2,1,0:T(8,128)(2,1)S(1)} all-gather(bf16[1,1,8,640]{3,2,1,0:T(8,128)(2,1)S(1)} %get-tuple-element.42), channel_id=3, replica_groups=mesh['section'=8,'dp'=16,'tensor'=4] {'dp'}, dimensions={2}, use_global_device_ids=true | all-gather | bytes 174080 | tf_op jit(solution)/shard_map/all_gather | solution.py:125
  78.2 15.2 %all-gather.2 = bf16[1,1,128,640]{3,2,1,0:T(8,128)(2,1)S(1)} all-gather(bf16[1,1,8,640]{3,2,1,0:T(8,128)(2,1)S(1)} %get-tuple-element.43), channel_id=4, replica_groups=mesh['section'=8,'dp'=16,'tensor'=4] {'dp'}, dimensions={2}, use_global_device_ids=true | all-gather | bytes 174080 | tf_op jit(solution)/shard_map/all_gather | solution.py:125
  100.5 18.1 %all-gather = bf16[1,128,640]{2,1,0:T(8,128)(2,1)S(1)} all-gather(bf16[1,8,640]{2,1,0:T(8,128)(2,1)S(1)} %copy-done.9), channel_id=2, replica_groups=mesh['section'=8,'dp'=16,'tensor'=4] {'dp'}, dimensions={1}, use_global_device_ids=true | all-gather | bytes 174080 | tf_op jit(solution)/shard_map/all_gather | solution.py:93
  118.8 9.3 %all-reduce.6 = (f32[128]{0:T(128)S(1)}, f32[128]{0:T(128)S(1)}) all-reduce(f32[128]{0:T(128)S(1)} %get-tuple-element.39, f32[128]{0:T(128)S(1)} %get-tuple-element.44), channel_id=1, replica_groups=mesh['section'=8,'dp'=16,'tensor'=4] {'tensor'}, use_global_device_ids=true, to_apply=%region_18.20 | all-reduce | flops 256 | bytes 2048 | tf_op jit(solution)/shard_map/psum | solution.py:136
  128.0 28.9 %all-reduce.32.cloned.1.call-done = (f32[128,896]{1,0:T(8,128)}, f32[128,896]{1,0:T(8,128)}) async-done(((f32[128,896]{1,0:T(8,128)}, f32[128,896]{1,0:T(8,128)}), (f32[128,896]{1,0:T(8,128)}, f32[128,896]{1,0:T(8,128)})) %all-reduce.32.cloned.1.call-update) | async-done | bytes 917520 | tf_op jit(solution)/shard_map/psum | solution.py:136
  156.9 2.2 multiply_reduce_fusion.1
  167.3 26.3 %all-reduce.3 = f32[128]{0:T(128)S(1)} all-reduce(f32[128]{0:T(128)S(1)} %get-tuple-element.31), channel_id=8, replica_groups=mesh['section'=8,'dp'=16,'tensor'=4] {'dp'}, use_global_device_ids=true, to_apply=%region_14.16.clone | all-reduce | flops 128 | bytes 1024
  193.7 82.5 %all-reduce.26.cloned.1.call-done = f32[128,640]{1,0:T(8,128)} async-done(((f32[128,640]{1,0:T(8,128)}), f32[128,640]{1,0:T(8,128)}) %all-reduce.26.cloned.1.call-update) | async-done | bytes 327696
  278.2 3.1 collective-permute-done.16
  283.7 2.1 collective-permute-start.18
  285.8 2.2 collective-permute-done.18
  289.0 3.3 collective-permute-done.19
  292.9 3.7 collective-permute-done.20
  297.2 3.8 collective-permute-done.21
  301.5 3.7 collective-permute-done.22
  305.4 8.4 %psum.71 = bf16[128]{0:T(256)(128)(2,1)S(1)} all-reduce(bf16[128]{0:T(256)(128)(2,1)S(1)} %fusion.21), channel_id=1, replica_groups=mesh['section'=8,'dp'=16,'tensor'=4] {'tensor'}, use_global_device_ids=true, to_apply=%region_2.3 | all-reduce | flops 128 | bytes 512 | tf_op jit(solution)/shard_map/psum | solution.py:99
  314.6 5.5 collective-permute-done.24
  320.2 4.2 collective-permute-done.25
  324.4 4.3 collective-permute-done.26
  329.4 3.7 collective-permute-done.27
  333.1 4.3 collective-permute-done.28
  338.0 3.7 collective-permute-done.29
  342.2 3.8 collective-permute-done.30
  348.1 2.2 collective-permute-done.31
  352.5 104.4 %all-reduce.22.cloned.1.call-done = bf16[128,640]{1,0:T(8,128)(2,1)} async-done(((bf16[128,640]{1,0:T(8,128)(2,1)}), bf16[128,640]{1,0:T(8,128)(2,1)}) %all-reduce.22.cloned.1.call-update) | async-done | bytes 163856
  457.7 3.1 collective-permute-start
  463.9 16.2 %all_gather.13 = bf16[128,640]{1,0:T(8,128)(2,1)S(1)} all-gather(bf16[8,640]{1,0:T(8,128)(2,1)S(1)} %bitcast_select_fusion.2), channel_id=1, replica_groups=mesh['section'=8,'dp'=16,'tensor'=4] {'dp'}, dimensions={0}, use_global_device_ids=true | all-gather | bytes 174080 | tf_op jit(solution)/shard_map/all_gather | solution.py:93
  487.9 24.6 %all-reduce.30.cloned.1.call-done = (f32[128,896]{1,0:T(8,128)}, f32[128,896]{1,0:T(8,128)}) async-done(((f32[128,896]{1,0:T(8,128)}, f32[128,896]{1,0:T(8,128)}), (f32[128,896]{1,0:T(8,128)}, f32[128,896]{1,0:T(8,128)})) %all-reduce.30.cloned.1.call-update) | async-done | bytes 917520 | tf_op jit(solution)/shard_map/psum | solution.py:136
  512.5 2.1 multiply_reduce_fusion
  526.1 2.5 select_select_fusion
  528.5 9.7 %all-to-all-start = ((f32[16,128,128]{2,1,0:T(8,128)}), f32[16,128,128]{2,1,0:T(8,128)}, u32[]{:S(2)}, u32[]{:S(2)}) async-start(f32[16,128,128]{2,1,0:T(8,128)} %select_select_fusion), calls=%async_computation | async-start | bytes 2097152 | tf_op jit(solution)/shard_map/all_to_all | solution.py:184
  539.7 8.5 %psum.73 = bf16[128]{0:T(256)(128)(2,1)S(1)} all-reduce(bf16[128]{0:T(256)(128)(2,1)S(1)} %fusion.19), channel_id=1, replica_groups=mesh['section'=8,'dp'=16,'tensor'=4] {'tensor'}, use_global_device_ids=true, to_apply=%region_6.7 | all-reduce | flops 128 | bytes 512 | tf_op jit(solution)/shard_map/psum | solution.py:99
  548.3 43.6 %all-reduce.20.cloned.1.call-done = bf16[128,896]{1,0:T(8,128)(2,1)} async-done(((bf16[128,896]{1,0:T(8,128)(2,1)}), bf16[128,896]{1,0:T(8,128)(2,1)}) %all-reduce.20.cloned.1.call-update) | async-done | bytes 229392 | tf_op jit(solution)/shard_map/psum | solution.py:98
  594.0 111.8 %all-reduce.24.cloned.1.call-done = bf16[128,640]{1,0:T(8,128)(2,1)} async-done(((bf16[128,640]{1,0:T(8,128)(2,1)}), bf16[128,640]{1,0:T(8,128)(2,1)}) %all-reduce.24.cloned.1.call-update) | async-done | bytes 163856
  708.4 23.2 %all-reduce.5 = f32[128]{0:T(128)S(1)} all-reduce(f32[128]{0:T(128)S(1)} %copy-done.16), channel_id=10, replica_groups=mesh['section'=8,'dp'=16,'tensor'=4] {'dp'}, use_global_device_ids=true, to_apply=%region_21.23.clone | all-reduce | flops 128 | bytes 1024
  731.6 89.3 %all-reduce.28.cloned.1.call-done = f32[128,640]{1,0:T(8,128)} async-done(((f32[128,640]{1,0:T(8,128)}), f32[128,640]{1,0:T(8,128)}) %all-reduce.28.cloned.1.call-update) | async-done | bytes 327696
  (217 shorter events, 65.4 us)
Async XLA Ops:
  7.2 149.8 %all-reduce.32.cloned.1.call-start = ((), (), s32[]{:S(2)}) async-start(), calls=%async_computation.8 | async-start | bytes 1835008 | tf_op jit(solution)/shard_map/psum | solution.py:136
  7.2 7.8 collective-permute-start.1
  15.0 4.5 collective-permute-start.2
  19.5 4.3 collective-permute-start.3
  23.8 4.3 collective-permute-start.4
  28.1 4.3 collective-permute-start.5
  32.4 4.3 collective-permute-start.6
  36.7 4.3 collective-permute-start.7
  41.0 4.3 collective-permute-start.8
  45.3 4.3 collective-permute-start.9
  49.6 4.3 collective-permute-start.10
  53.9 4.3 collective-permute-start.11
  58.2 18.1 %collective-permute-start.12 = (bf16[8,640]{1,0:T(8,128)(2,1)S(1)}, bf16[8,640]{1,0:T(8,128)(2,1)S(1)}, u32[]{:S(2)}, u32[]{:S(2)}) collective-permute-start(bf16[8,640]{1,0:T(8,128)(2,1)S(1)} %collective-permute-done.11), channel_id=1, source_target_pairs={{0,4},{4,8},{8,12},{12,16},{16,20},{20,24},{24,28},{28,32},{32,36}... | collective-permute-start | bytes 30728 | tf_op jit(solution)/shard_map/ppermute | solution.py:128
  76.3 17.4 %collective-permute-start.13 = (bf16[8,640]{1,0:T(8,128)(2,1)S(1)}, bf16[8,640]{1,0:T(8,128)(2,1)S(1)}, u32[]{:S(2)}, u32[]{:S(2)}) collective-permute-start(bf16[8,640]{1,0:T(8,128)(2,1)S(1)} %collective-permute-done.12), channel_id=1, source_target_pairs={{0,4},{4,8},{8,12},{12,16},{16,20},{20,24},{24,28},{28,32},{32,36}... | collective-permute-start | bytes 30728 | tf_op jit(solution)/shard_map/ppermute | solution.py:128
  93.7 1.2 collective-permute-start.14
  94.9 4.0 collective-permute-start.15
  100.5 175.7 %all-reduce.26.cloned.1.call-start = ((), (), s32[]{:S(2)}) async-start(), calls=%async_computation.5 | async-start | bytes 655360
  160.3 185.7 %all-reduce.18.cloned.1.call-start = ((), (), s32[]{:S(2)}) async-start(), calls=%async_computation.1 | async-start | bytes 458752 | tf_op jit(solution)/shard_map/psum | solution.py:98
  161.6 114.5 %copy-start.7 = (bf16[1,2,8,640]{3,2,1,0:T(8,128)(2,1)S(1)}, bf16[1,2,8,640]{3,2,1,0:T(8,128)(2,1)}, u32[]{:S(2)}) copy-start(bf16[1,2,8,640]{3,2,1,0:T(8,128)(2,1)} %param.23) | copy-start | bytes 61444
  161.6 119.7 %copy-start.11 = (bf16[1,8,640]{2,1,0:T(8,128)(2,1)S(1)}, bf16[1,8,640]{2,1,0:T(8,128)(2,1)}, u32[]{:S(2)}) copy-start(bf16[1,8,640]{2,1,0:T(8,128)(2,1)} %param.21) | copy-start | bytes 30724
  161.7 295.3 %all-reduce.22.cloned.1.call-start = ((), (), s32[]{:S(2)}) async-start(), calls=%async_computation.3 | async-start | bytes 327680
  276.9 4.4 collective-permute-start.16
  281.4 2.3 collective-permute-start.17
  283.7 4.3 collective-permute-start.18
  288.0 4.3 collective-permute-start.19
  292.3 4.3 collective-permute-start.20
  296.6 4.3 collective-permute-start.21
  301.0 4.3 collective-permute-start.22
  305.3 8.5 %collective-permute-start.23 = (bf16[8,640]{1,0:T(8,128)(2,1)S(1)}, bf16[8,640]{1,0:T(8,128)(2,1)S(1)}, u32[]{:S(2)}, u32[]{:S(2)}) collective-permute-start(bf16[8,640]{1,0:T(8,128)(2,1)S(1)} %collective-permute-done.22), channel_id=1, source_target_pairs={{0,4},{4,8},{8,12},{12,16},{16,20},{20,24},{24,28},{28,32},{32,36}... | collective-permute-start | bytes 30728 | tf_op jit(solution)/shard_map/ppermute | solution.py:128
  313.8 6.3 collective-permute-start.24
  320.1 4.3 collective-permute-start.25
  324.4 4.3 collective-permute-start.26
  328.7 4.3 collective-permute-start.27
  333.0 4.3 collective-permute-start.28
  337.4 4.3 collective-permute-start.29
  341.7 4.3 collective-permute-start.30
  346.0 4.3 collective-permute-start.31
  348.0 164.4 %all-reduce.30.cloned.1.call-start = ((), (), s32[]{:S(2)}) async-start(), calls=%async_computation.7 | async-start | bytes 1835008 | tf_op jit(solution)/shard_map/psum | solution.py:136
  457.7 6.2 collective-permute-start
  528.5 293.8 %all-to-all-start = ((f32[16,128,128]{2,1,0:T(8,128)}), f32[16,128,128]{2,1,0:T(8,128)}, u32[]{:S(2)}, u32[]{:S(2)}) async-start(f32[16,128,128]{2,1,0:T(8,128)} %select_select_fusion), calls=%async_computation | async-start | bytes 2097152 | tf_op jit(solution)/shard_map/all_to_all | solution.py:184
  538.2 53.7 %all-reduce.20.cloned.1.call-start = ((), (), s32[]{:S(2)}) async-start(), calls=%async_computation.2 | async-start | bytes 458752 | tf_op jit(solution)/shard_map/psum | solution.py:98
  539.6 166.3 %all-reduce.24.cloned.1.call-start = ((), (), s32[]{:S(2)}) async-start(), calls=%async_computation.4 | async-start | bytes 327680
  593.9 137.6 %copy-start.15 = (f32[128]{0:T(128)S(1)}, f32[128]{0:T(128)}, u32[]{:S(2)}) copy-start(f32[128]{0:T(128)} %add_rsqrt_fusion) | copy-start | bytes 1540
  594.0 227.0 %all-reduce.28.cloned.1.call-start = ((), (), s32[]{:S(2)}) async-start(), calls=%async_computation.6 | async-start | bytes 655360
  706.5 117.6 %copy-start.5 = (f32[1,1,1,6,128,128]{5,4,3,2,1,0:T(8,128)S(1)}, f32[1,1,1,6,128,128]{5,4,3,2,1,0:T(8,128)}, u32[]{:S(2)}) copy-start(f32[1,1,1,6,128,128]{5,4,3,2,1,0:T(8,128)} %param.30) | copy-start | bytes 1179652
  706.5 117.6 %copy-start.6 = (f32[1,1,1,6,128,128]{5,4,3,2,1,0:T(8,128)S(1)}, f32[1,1,1,6,128,128]{5,4,3,2,1,0:T(8,128)}, u32[]{:S(2)}) copy-start(f32[1,1,1,6,128,128]{5,4,3,2,1,0:T(8,128)} %param.31) | copy-start | bytes 1179652
  706.5 117.6 %copy-start.18 = (pred[6]{0:T(512)(128)(4,1)S(1)}, pred[6]{0:T(512)(128)(4,1)}, u32[]{:S(2)}) copy-start(pred[6]{0:T(512)(128)(4,1)} %compare_and_fusion.3) | copy-start | bytes 22
  706.6 117.6 %copy-start.19 = (pred[6]{0:T(512)(128)(4,1)S(1)}, pred[6]{0:T(512)(128)(4,1)}, u32[]{:S(2)}) copy-start(pred[6]{0:T(512)(128)(4,1)} %fusion.67) | copy-start | bytes 22
  (16 other events, 408.5 us)
Sparse Core Ops, SparseCore 0:
  100.6 56.3 all-reduce.31
  160.4 115.6 all-reduce.25
  279.1 49.1 all-reduce.17
  348.2 108.7 all-reduce.21
  459.3 53.0 all-reduce.29
  541.8 50.0 all-reduce.19
  594.8 110.9 all-reduce.23
  708.8 112.0 all-reduce.27
